TPU v7x, 32 devices: a whole 2x2x4 slice. The times are simulated.
32 devices in a mesh: tm: 8 (over z, x), lev: 4 (over y, core).
Axes of the slice: x: 2, y: 2, z: 4, core: 2. Of those that a mesh axis runs over, the one named last changes fastest.
Arguments:
- fields: bfloat16 [4, 32, 9, 16384], P('lev', 'tm'), may hold values from -18 to 18
- lengths: int32 [8], P('tm'), may hold values from 1 to 4, 24 in all
- owners: int32 [9], replicated, may hold values from 0 to 7, as said below
- thickness: float32 [4], replicated, may hold values from 0.2 to 5
Outputs:
- daily_means: float32 [4, 16, 1, 16384], P('lev', 'tm')
- column_means: float32 [16, 1, 16384], P('tm', None, 'lev')
Inputs may be any that keep to these rules, and one draw needn't show every extreme that they name: `lengths`: the entries sum to 24 and the largest is exactly 4. `owners`: no index owns more than 2 tiles; some index owns exactly 2.
All inputs are finite; a program needn't handle non-finite values. No bound on the sum of `lengths` on one device may be relied on, other than what follows from the above.
Results may differ from a plain program's by a relative error of at most 0.0003.
Values may be sent and summed in bfloat16 or wider, within the bound.
No kernel may reach another device: no remote copies, remote signals or barrier semaphores. Data moves between devices by JAX's collectives and lax.ppermute only.
A program may use at most 128 MiB of HBM per device.

v0:
```python
import jax
import jax.numpy as jnp
from jax import lax
from jax.sharding import PartitionSpec as P

MAXT = 2
HOURS_DEV = 3


def slot_table(owners, slot_total):
    tile_count = owners.shape[0]
    tile_ids = jnp.arange(tile_count, dtype=jnp.int32)
    earlier = (owners[None, :] == owners[:, None]) & (tile_ids[None, :] < tile_ids[:, None])
    tile_rank = jnp.sum(earlier.astype(jnp.int32), axis=1)
    position = owners * MAXT + tile_rank
    slot_ids = jnp.arange(slot_total, dtype=jnp.int32)
    matches = (position[None, :] == slot_ids[:, None]).astype(jnp.int32)
    tile_of = jnp.sum(matches * tile_ids[None, :], axis=1)
    slot_valid = jnp.sum(matches, axis=1)
    return (tile_of, slot_valid)


def local(fields, lengths, owners, thickness):
    local_block = fields[0]
    slot_count = local_block.shape[0]
    devices = lax.axis_size("tm")
    my_index = lax.axis_index("tm")
    all_lengths = lax.all_gather(lengths, "tm", axis=0, tiled=True)
    offsets = jnp.cumsum(all_lengths) - all_lengths
    tile_of, slot_valid = slot_table(owners, devices * MAXT)
    own_slots = lax.dynamic_slice_in_dim(slot_valid, my_index * MAXT, MAXT, 0).astype(jnp.float32)
    day_ids = jnp.arange(devices * HOURS_DEV // 24, dtype=jnp.int32)
    row_ids = jnp.arange(devices * slot_count, dtype=jnp.int32)
    source_ids = row_ids // slot_count
    slot_ids = row_ids % slot_count
    hour_of = offsets[source_ids] + slot_ids
    is_valid = slot_ids < all_lengths[source_ids]
    select = (is_valid[:, None] & (hour_of[:, None] // 24 == day_ids[None, :])).astype(jnp.bfloat16)
    outgoing = jnp.take(local_block, tile_of, axis=1)
    period_means = (
        jnp.einsum(
            "rd,rmc->mdc",
            select,
            lax.all_to_all(outgoing, "tm", split_axis=1, concat_axis=0, tiled=True),
            preferred_element_type=jnp.float32,
        )
        / 24.0
    )
    period_means = period_means * own_slots[:, None, None]
    my_level = lax.axis_index("lev")
    fraction = thickness[my_level] / jnp.sum(thickness)
    weighted = fraction * period_means
    column_sum = lax.psum(weighted, "lev")
    share = column_sum.shape[2] // lax.axis_size("lev")
    column_part = lax.dynamic_slice_in_dim(column_sum, my_level * share, share, 2)
    return (period_means[None], column_part)


def solution(mesh):
    placed = (P("lev", "tm", None, None), P("tm"), P(), P())
    return jax.shard_map(
        local,
        mesh=mesh,
        in_specs=placed,
        out_specs=(P("lev", "tm", None, None), P("tm", None, "lev")),
        check_vma=False,
    )
```

profile of v0, /device:TPU:0, one launch (start us, length us, event | category | flops | bytes accessed | tf_op | source)
XLA Modules:
  0.0 117.4 jit_solution(15610676181587338304)
XLA Ops:
  7.2 0.9 convert_reduce_fusion.1
  8.1 0.7 multiply_add_fusion
  8.8 0.1 convert_reduce_fusion
  8.9 2.4 %gather_fusion = bf16[16,4,16384]{2,1,0:T(4,128)(2,1)S(1)} fusion(bf16[4,9,16384]{2,0,1:T(4,128)(2,1)S(1)} %bitcast.24, s32[1024]{0:T(1024)S(1)} %pad_clamp_fusion.1), kind=kCustom, calls=%fused_computation | custom fusion | bytes 4194368 | tf_op jit(solution)/shard_map/jit(_take)/gather | solution.py:39
  11.3 2.3 %select_bitcast_fusion = bf16[4,16,16384]{2,0,1:T(4,128)(2,1)} fusion(bf16[16,4,16384]{2,1,0:T(4,128)(2,1)S(1)} %gather_fusion, pred[16]{0:T(512)(128)(4,1)S(1)} %compare_and_fusion), kind=kLoop, calls=%fused_computation.5 | loop fusion | flops 1048576 | bytes 4194320 | tf_op jit(solution)/shard_map/jit(_take)/select_n | solution.py:39
  13.7 7.4 %all-to-all-start = ((bf16[4,16,16384]{2,0,1:T(4,128)(2,1)}), bf16[4,16,16384]{2,0,1:T(4,128)(2,1)S(1)}, u32[]{:S(2)}, u32[]{:S(2)}) async-start(bf16[4,16,16384]{2,0,1:T(4,128)(2,1)} %select_bitcast_fusion), calls=%async_computation | async-start | bytes 4194304 | tf_op jit(solution)/shard_map/all_to_all | solution.py:44
  21.1 0.0 all-reduce.3.cloned.1.call-start
  21.8 0.6 dynamic-slice
  22.4 0.8 dynamic-update-slice
  23.1 46.4 %all-reduce = s32[8]{0:T(128)S(1)} all-reduce(s32[8]{0:T(128)S(1)} %dynamic-update-slice), channel_id=1, replica_groups=mesh['tm'=8,'lev'=4] {'tm'}, use_global_device_ids=true, to_apply=%add | all-reduce | flops 8 | bytes 64
  69.5 0.6 dynamic_slice.10
  70.1 0.6 reduce_sum.42
  70.7 0.7 gather_fusion.1
  71.4 0.2 reduce-window.9
  71.6 0.7 gather_fusion.2
  73.6 0.1 convert_multiply_fusion
  73.7 2.2 %copy.7 = bf16[4,8,2,16384]{3,2,0,1:T(2,128)(2,1)S(1)} copy(bf16[4,8,2,16384]{3,0,2,1:T(4,128)(2,1)S(1)} %bitcast.26) | data formatting | bytes 4194304 | tf_op jit(solution)/shard_map/all_to_all | solution.py:44
  75.9 1.3 %fusion = f32[1,2,16384]{2,0,1:T(1,128)S(1)} fusion(bf16[32,2,16384]{2,1,0:T(2,128)(2,1)S(1)} %bitcast.27, s32[32]{0:T(128)S(1)} %gather_fusion.1, s32[32]{0:T(128)S(1)} %gather_fusion.2), kind=kOutput, calls=%fused_computation.3 | convolution fusion | flops 2097728 | bytes 2228480 | tf_op jit(solution)/shard_map/rd,rmc->mdc/dot_general | solution.py:41
  77.2 0.2 broadcast_multiply_fusion
  77.4 0.7 mul.49
  78.1 0.0 all-reduce.3.cloned.1.call-update
  78.1 0.7 broadcast_in_dim.11
  78.9 30.3 %all-reduce.3.cloned.1.call-done = f32[2,1,16384]{2,1,0:T(1,128)} async-done(((f32[2,1,16384]{2,1,0:T(1,128)}), f32[2,1,16384]{2,1,0:T(1,128)}) %all-reduce.3.cloned.1.call-update) | async-done | bytes 131088 | tf_op jit(solution)/shard_map/psum | solution.py:53
  109.2 1.4 %constant_dynamic-slice_fusion = f32[2,1,4096]{2,1,0:T(1,128)} fusion(f32[2,1,16384]{2,1,0:T(1,128)} %all-reduce.3.cloned.1.call-done, s32[]{:T(128)S(6)} %select_n.84), kind=kLoop, calls=%fused_computation.46 | loop fusion | bytes 65540 | tf_op jit(solution)/shard_map/dynamic_slice | solution.py:55
  (14 shorter events, 0.1 us)
Async XLA Ops:
  7.2 1.8 %copy-start = (bf16[1,4,9,16384]{3,1,2,0:T(4,128)(2,1)S(1)}, bf16[1,4,9,16384]{3,1,2,0:T(4,128)(2,1)}, u32[]{:S(2)}) copy-start(bf16[1,4,9,16384]{3,1,2,0:T(4,128)(2,1)} %param.4) | copy-start | bytes 3538948
  13.7 8.1 %copy-start.2 = (u32[32]{0:T(128)S(1)}, u32[32]{0:T(128)}, u32[]{:S(2)}) copy-start(u32[32]{0:T(128)} %constant.88) | copy-start | bytes 388
  13.7 55.8 %copy-start.1 = (f32[4]{0:T(128)S(1)}, f32[4]{0:T(128)}, u32[]{:S(2)}) copy-start(f32[4]{0:T(128)} %param.7) | copy-start | bytes 52
  13.7 60.1 %all-to-all-start = ((bf16[4,16,16384]{2,0,1:T(4,128)(2,1)}), bf16[4,16,16384]{2,0,1:T(4,128)(2,1)S(1)}, u32[]{:S(2)}, u32[]{:S(2)}) async-start(bf16[4,16,16384]{2,0,1:T(4,128)(2,1)} %select_bitcast_fusion), calls=%async_computation | async-start | bytes 4194304 | tf_op jit(solution)/shard_map/all_to_all | solution.py:44
  21.1 88.1 %all-reduce.3.cloned.1.call-start = ((), (), s32[]{:S(2)}) async-start(), calls=%async_computation.1 | async-start | bytes 262144 | tf_op jit(solution)/shard_map/psum | solution.py:53
Sparse Core Ops, SparseCore 0:
  78.3 30.8 all-reduce.2
where the time goes:
time: 118 us; the launch traced here: 117 us
  blocking collectives  46.4 us (39%)
  waiting for transfers between devices  30.3 us (26%)
  between operations  16.1 us (14%)
  local copies, waits for them, and re-layouts  10.7 us (9%)
  starting transfers between devices  7.45 us (6%)
  other arithmetic  5.17 us (4%)
  matrix products  1.25 us (1%)
    unnamed x1, blocking collectives  46.4 us
    psum x1, waiting for transfers between devices, local(): column_sum = lax.psum(weighted, 'lev')  30.3 us
    all_to_all x1, starting transfers between devices, local(): lax.all_to_all(outgoing, 'tm', split_axis=1, concat_axis=0, tiled=True)  7.41 us
    gather x1, local copies, waits for them, and re-layouts, local(): outgoing = jnp.take(local_block, tile_of, axis=1)  2.36 us
  transfers between devices with their start and end apart: 2, of which 1 were waited for; matrix products, arithmetic and copies ran while one was open for 4% of the time, Pallas kernels for 0%

commit v1 on v0

--- a/solution.py
+++ b/solution.py
@@ -50,7 +50,8 @@
     my_level = lax.axis_index("lev")
     fraction = thickness[my_level] / jnp.sum(thickness)
     weighted = fraction * period_means
-    column_sum = lax.psum(weighted, "lev")
+    pieces = lax.all_gather(weighted, "lev", axis=0, tiled=False)
+    column_sum = pieces.sum(axis=0)
     share = column_sum.shape[2] // lax.axis_size("lev")
     column_part = lax.dynamic_slice_in_dim(column_sum, my_level * share, share, 2)
     return (period_means[None], column_part)

time: 118 us -> 80 us (0.68)
  waiting for transfers between devices: 30.3 us -> 0.01 us
  between operations: 16.1 us -> 2.71 us
  blocking collectives: 46.4 us -> 53.6 us
  local copies, waits for them, and re-layouts: 10.7 us -> 9.33 us
    psum x1 -> x0, waiting for transfers between devices: 30.3 us -> none  [local(): column_sum = lax.psum(weighted, 'lev')]
    all_gather x0 -> x1, blocking collectives: none -> 7.18 us  [local(): pieces = lax.all_gather(weighted, 'lev', axis=0, tiled=False)]
  transfers between devices with their start and end apart: 2 -> 1, of which waited for: 1 -> 0; matrix products, arithmetic and copies ran while one was open for 4% -> 5% of each run, Pallas kernels for 0% -> 0%
where the time goes in v1:
time: 80 us; the launch traced here: 79.7 us
  blocking collectives  53.6 us (67%)
  local copies, waits for them, and re-layouts  9.33 us (12%)
  starting transfers between devices  7.41 us (9%)
  other arithmetic  5.42 us (7%)
  between operations  2.71 us (3%)
  matrix products  1.25 us (2%)
    unnamed x1, blocking collectives  46.4 us
    all_to_all x1, starting transfers between devices, local(): lax.all_to_all(outgoing, 'tm', split_axis=1, concat_axis=0, tiled=True)  7.41 us
    all_gather x1, blocking collectives, local(): pieces = lax.all_gather(weighted, 'lev', axis=0, tiled=False)  7.18 us
    gather x1, local copies, waits for them, and re-layouts, local(): outgoing = jnp.take(local_block, tile_of, axis=1)  2.36 us
    select_n x2, other arithmetic, local(): outgoing = jnp.take(local_block, tile_of, axis=1)  2.35 us
    all_to_all x1, local copies, waits for them, and re-layouts, local(): lax.all_to_all(outgoing, 'tm', split_axis=1, concat_axis=0, tiled=True)  2.18 us
    unnamed x10, local copies, waits for them, and re-layouts  2.15 us
  transfers between devices with their start and end apart: 1, of which 0 were waited for; matrix products, arithmetic and copies ran while one was open for 5% of the time, Pallas kernels for 0%

profile of v1, /device:TPU:0, one launch (start us, length us, event | category | flops | bytes accessed | tf_op | source)
XLA Modules:
  0.0 79.7 jit_solution(5785995772954199772)
XLA Ops:
  0.6 0.0 copy-start
  0.6 0.9 %convert_reduce_fusion.1 = s32[9]{0:T(128)S(1)} fusion(s32[9]{0:T(128)} %param.6), kind=kLoop, calls=%fused_computation.12 | loop fusion | flops 396 | bytes 72 | tf_op jit(solution)/shard_map/reduce_sum | solution.py:14
  1.6 0.7 multiply_add_fusion
  2.3 0.1 convert_reduce_fusion
  2.4 2.4 %gather_fusion = bf16[16,4,16384]{2,1,0:T(4,128)(2,1)S(1)} fusion(bf16[4,9,16384]{2,0,1:T(4,128)(2,1)S(1)} %bitcast.31, s32[1024]{0:T(1024)S(1)} %pad_clamp_fusion.1), kind=kCustom, calls=%fused_computation | custom fusion | bytes 4194368 | tf_op jit(solution)/shard_map/jit(_take)/gather | solution.py:39
  4.8 2.3 %select_bitcast_fusion = bf16[4,16,16384]{2,0,1:T(4,128)(2,1)} fusion(bf16[16,4,16384]{2,1,0:T(4,128)(2,1)S(1)} %gather_fusion, pred[16]{0:T(512)(128)(4,1)S(1)} %compare_and_fusion), kind=kLoop, calls=%fused_computation.5 | loop fusion | flops 1048576 | bytes 4194320 | tf_op jit(solution)/shard_map/jit(_take)/select_n | solution.py:39
  7.1 7.4 %all-to-all-start = ((bf16[4,16,16384]{2,0,1:T(4,128)(2,1)}), bf16[4,16,16384]{2,0,1:T(4,128)(2,1)S(1)}, u32[]{:S(2)}, u32[]{:S(2)}) async-start(bf16[4,16,16384]{2,0,1:T(4,128)(2,1)} %select_bitcast_fusion), calls=%async_computation | async-start | bytes 4194304 | tf_op jit(solution)/shard_map/all_to_all | solution.py:44
  15.2 0.6 dynamic-slice.4
  15.8 0.8 dynamic-update-slice
  16.6 46.4 %all-reduce = s32[8]{0:T(128)S(1)} all-reduce(s32[8]{0:T(128)S(1)} %dynamic-update-slice), channel_id=1, replica_groups=mesh['tm'=8,'lev'=4] {'tm'}, use_global_device_ids=true, to_apply=%add | all-reduce | flops 8 | bytes 64
  63.0 0.7 gather_fusion.1
  63.7 0.2 reduce-window.9
  63.9 0.7 gather_fusion.2
  64.6 0.6 dynamic_slice.10
  65.2 0.6 reduce_sum.51
  67.1 0.1 convert_multiply_fusion
  67.2 0.0 all-to-all-done
  67.2 2.2 %copy.9 = bf16[4,8,2,16384]{3,2,0,1:T(2,128)(2,1)S(1)} copy(bf16[4,8,2,16384]{3,0,2,1:T(4,128)(2,1)S(1)} %bitcast.33) | data formatting | bytes 4194304 | tf_op jit(solution)/shard_map/all_to_all | solution.py:44
  69.4 1.3 %fusion = f32[1,2,16384]{2,0,1:T(1,128)S(1)} fusion(bf16[32,2,16384]{2,1,0:T(2,128)(2,1)S(1)} %bitcast.34, s32[32]{0:T(128)S(1)} %gather_fusion.1, s32[32]{0:T(128)S(1)} %gather_fusion.2), kind=kOutput, calls=%fused_computation.3 | convolution fusion | flops 2097728 | bytes 2228480 | tf_op jit(solution)/shard_map/rd,rmc->mdc/dot_general | solution.py:41
  70.6 0.2 multiply_bitcast_fusion
  70.8 0.8 copy.10
  71.6 7.2 %all-gather.1 = f32[4,2,16384]{2,1,0:T(2,128)S(1)} all-gather(f32[1,2,16384]{2,1,0:T(2,128)S(1)} %get-tuple-element.8), channel_id=2, replica_groups=mesh['tm'=8,'lev'=4] {'lev'}, dimensions={0}, use_global_device_ids=true | all-gather | bytes 655360 | tf_op jit(solution)/shard_map/all_gather | solution.py:53
  78.8 0.3 reduce.1
  79.1 0.6 dynamic_slice.11
  (13 shorter events, 0.1 us)
Async XLA Ops:
  0.6 1.8 %copy-start = (bf16[1,4,9,16384]{3,1,2,0:T(4,128)(2,1)S(1)}, bf16[1,4,9,16384]{3,1,2,0:T(4,128)(2,1)}, u32[]{:S(2)}) copy-start(bf16[1,4,9,16384]{3,1,2,0:T(4,128)(2,1)} %param.4) | copy-start | bytes 3538948
  7.1 8.1 %copy-start.2 = (u32[32]{0:T(128)S(1)}, u32[32]{0:T(128)}, u32[]{:S(2)}) copy-start(u32[32]{0:T(128)} %constant.88) | copy-start | bytes 388
  7.1 57.4 %copy-start.1 = (f32[4]{0:T(128)S(1)}, f32[4]{0:T(128)}, u32[]{:S(2)}) copy-start(f32[4]{0:T(128)} %param.7) | copy-start | bytes 52
  7.1 60.1 %all-to-all-start = ((bf16[4,16,16384]{2,0,1:T(4,128)(2,1)}), bf16[4,16,16384]{2,0,1:T(4,128)(2,1)S(1)}, u32[]{:S(2)}, u32[]{:S(2)}) async-start(bf16[4,16,16384]{2,0,1:T(4,128)(2,1)} %select_bitcast_fusion), calls=%async_computation | async-start | bytes 4194304 | tf_op jit(solution)/shard_map/all_to_all | solution.py:44

commit v2 on v0

--- a/solution.py
+++ b/solution.py
@@ -5,6 +5,13 @@
 
 MAXT = 2
 HOURS_DEV = 3
+
+
+def fields_edit(t0, pos_dim, array_axis):
+    return jnp.concatenate(
+        lax.all_to_all(jnp.stack(jnp.split(t0, lax.axis_size("tm"), pos_dim), axis=0), "tm", 0, 0),
+        axis=array_axis,
+    )
 
 
 def slot_table(owners, slot_total):
@@ -39,10 +46,7 @@
     outgoing = jnp.take(local_block, tile_of, axis=1)
     period_means = (
         jnp.einsum(
-            "rd,rmc->mdc",
-            select,
-            lax.all_to_all(outgoing, "tm", split_axis=1, concat_axis=0, tiled=True),
-            preferred_element_type=jnp.float32,
+            "rd,rmc->mdc", select, fields_edit(outgoing, 1, 0), preferred_element_type=jnp.float32
         )
         / 24.0
     )

time: 118 us -> 123 us (1.042)
  local copies, waits for them, and re-layouts: 10.7 us -> 17.1 us
  other arithmetic: 5.17 us -> 3.81 us
    unnamed x9 -> x16, local copies, waits for them, and re-layouts: 1.36 us -> 6.94 us
    select_n x2, other arithmetic: 2.35 us -> 1 us  [local(): outgoing = jnp.take(local_block, tile_of, axis=1)]
where the time goes in v2:
time: 123 us; the launch traced here: 122 us
  blocking collectives  46.4 us (38%)
  waiting for transfers between devices  30.3 us (25%)
  local copies, waits for them, and re-layouts  17.1 us (14%)
  between operations  16.1 us (13%)
  starting transfers between devices  7.45 us (6%)
  other arithmetic  3.81 us (3%)
  matrix products  1.25 us (1%)
    unnamed x1, blocking collectives  46.4 us
    psum x1, waiting for transfers between devices, local(): column_sum = lax.psum(weighted, 'lev')  30.3 us
    all_to_all x1, starting transfers between devices, fields_edit(): lax.all_to_all(jnp.stack(jnp.split(t0, lax.axis_size('tm'), pos_dim), axi...  7.41 us
    unnamed x16, local copies, waits for them, and re-layouts  6.94 us
  transfers between devices with their start and end apart: 2, of which 1 were waited for; matrix products, arithmetic and copies ran while one was open for 4% of the time, Pallas kernels for 0%

profile of v2, /device:TPU:0, one launch (start us, length us, event | category | flops | bytes accessed | tf_op | source)
XLA Modules:
  0.0 122.4 jit_solution(9852250350488496106)
XLA Ops:
  7.2 0.9 convert_reduce_fusion.1
  8.1 0.7 multiply_add_fusion
  8.9 2.4 %gather_fusion = bf16[16,4,16384]{2,1,0:T(4,128)(2,1)S(1)} fusion(bf16[4,9,16384]{2,0,1:T(4,128)(2,1)S(1)} %bitcast.53, s32[1024]{0:T(1024)S(1)} %pad_clamp_fusion.1), kind=kCustom, calls=%fused_computation | custom fusion | bytes 4194368 | tf_op jit(solution)/shard_map/jit(_take)/gather | solution.py:46
  11.3 1.0 select_bitcast_fusion
  12.3 0.8 fusion.9
  13.1 0.8 fusion.8
  13.9 0.8 fusion.7
  14.7 0.8 fusion.6
  15.5 0.8 fusion.5
  16.3 0.8 fusion.4
  17.1 0.8 fusion.3
  17.9 0.8 fusion.2
  18.7 7.4 %all-to-all-start = ((bf16[8,4,2,16384]{3,1,2,0:T(4,128)(2,1)}), bf16[8,4,2,16384]{3,1,2,0:T(4,128)(2,1)S(1)}, u32[]{:S(2)}, u32[]{:S(2)}) async-start(bf16[8,4,2,16384]{3,1,2,0:T(4,128)(2,1)} %fusion.2), calls=%async_computation | async-start | bytes 4194304 | tf_op jit(solution)/shard_map/all_to_all | solution.py:12
  27.4 0.8 dynamic-update-slice
  28.2 46.4 %all-reduce = s32[8]{0:T(128)S(1)} all-reduce(s32[8]{0:T(128)S(1)} %dynamic-update-slice), channel_id=1, replica_groups=mesh['tm'=8,'lev'=4] {'tm'}, use_global_device_ids=true, to_apply=%add | all-reduce | flops 8 | bytes 64
  74.7 0.7 gather_fusion.1
  75.4 0.7 gather_fusion.2
  76.7 0.6 reduce_sum.42
  78.8 2.2 %copy.7 = bf16[8,4,2,16384]{3,2,1,0:T(2,128)(2,1)S(1)} copy(bf16[8,4,2,16384]{3,1,2,0:T(4,128)(2,1)S(1)} %all-to-all-done) | data formatting | bytes 4194304 | tf_op jit(solution)/shard_map/all_to_all | solution.py:12
  80.9 1.3 %fusion = f32[1,2,16384]{2,0,1:T(1,128)S(1)} fusion(bf16[32,2,16384]{2,1,0:T(2,128)(2,1)S(1)} %bitcast.55, s32[32]{0:T(128)S(1)} %gather_fusion.1, s32[32]{0:T(128)S(1)} %gather_fusion.2), kind=kOutput, calls=%fused_computation.3 | convolution fusion | flops 2097728 | bytes 2228480 | tf_op jit(solution)/shard_map/rd,rmc->mdc/dot_general | solution.py:48
  82.4 0.7 mul.49
  83.2 0.7 broadcast_in_dim.11
  83.9 30.3 %all-reduce.3.cloned.1.call-done = f32[2,1,16384]{2,1,0:T(1,128)} async-done(((f32[2,1,16384]{2,1,0:T(1,128)}), f32[2,1,16384]{2,1,0:T(1,128)}) %all-reduce.3.cloned.1.call-update) | async-done | bytes 131088 | tf_op jit(solution)/shard_map/psum | solution.py:57
  114.2 1.4 %constant_dynamic-slice_fusion = f32[2,1,4096]{2,1,0:T(1,128)} fusion(f32[2,1,16384]{2,1,0:T(1,128)} %all-reduce.3.cloned.1.call-done, s32[]{:T(128)S(6)} %select_n.84), kind=kLoop, calls=%fused_computation.62 | loop fusion | bytes 65540 | tf_op jit(solution)/shard_map/dynamic_slice | solution.py:59
  (22 shorter events, 1.9 us)
Async XLA Ops:
  7.2 1.8 %copy-start = (bf16[1,4,9,16384]{3,1,2,0:T(4,128)(2,1)S(1)}, bf16[1,4,9,16384]{3,1,2,0:T(4,128)(2,1)}, u32[]{:S(2)}) copy-start(bf16[1,4,9,16384]{3,1,2,0:T(4,128)(2,1)} %param.4) | copy-start | bytes 3538948
  18.7 8.1 %copy-start.2 = (u32[32]{0:T(128)S(1)}, u32[32]{0:T(128)}, u32[]{:S(2)}) copy-start(u32[32]{0:T(128)} %constant.88) | copy-start | bytes 388
  18.7 57.4 %copy-start.1 = (f32[4]{0:T(128)S(1)}, f32[4]{0:T(128)}, u32[]{:S(2)}) copy-start(f32[4]{0:T(128)} %param.7) | copy-start | bytes 52
  18.7 60.1 %all-to-all-start = ((bf16[8,4,2,16384]{3,1,2,0:T(4,128)(2,1)}), bf16[8,4,2,16384]{3,1,2,0:T(4,128)(2,1)S(1)}, u32[]{:S(2)}, u32[]{:S(2)}) async-start(bf16[8,4,2,16384]{3,1,2,0:T(4,128)(2,1)} %fusion.2), calls=%async_computation | async-start | bytes 4194304 | tf_op jit(solution)/shard_map/all_to_all | solution.py:12
  26.1 88.1 %all-reduce.3.cloned.1.call-start = ((), (), s32[]{:S(2)}) async-start(), calls=%async_computation.1 | async-start | bytes 262144 | tf_op jit(solution)/shard_map/psum | solution.py:57
Sparse Core Ops, SparseCore 0:
  83.3 30.8 all-reduce.2
